TPU v7x, 32 devices: a whole 2x2x4 slice. The times are simulated.
32 devices in a mesh: parts: 2 (over y), seq: 16 (over z, x, core).
Axes of the slice: x: 2, y: 2, z: 4, core: 2. Of those that a mesh axis runs over, the one named last changes fastest.
Arguments:
- queries: bfloat16 [32, 8192], P(('parts', 'seq')), parts along dimension 0, may hold values from -140 to 140
- new_keys: bfloat16 [32, 1024], P(('parts', 'seq')), parts along dimension 0, may hold values from -7 to 7
- new_values: bfloat16 [32, 1024], P(('parts', 'seq')), parts along dimension 0, may hold values from -6 to 6
- doc_keys: bfloat16 [32768, 1024], P(('parts', 'seq')), parts along dimension 0, may hold values from -6 to 6
- doc_values: bfloat16 [32768, 1024], P(('parts', 'seq')), parts along dimension 0, may hold values from -6 to 6
- suffix_keys: bfloat16 [32768, 1024], P(('parts', 'seq')), parts along dimension 0, may hold values from -6 to 6
- suffix_values: bfloat16 [32768, 1024], P(('parts', 'seq')), parts along dimension 0, may hold values from -6 to 6
- keep_lists: int32 [32, 32], P(('parts', 'seq')), parts along dimension 0, may hold values from 0 to 127, as said below
- suffix_lengths: int32 [16], P('parts'), parts along dimension 0, may hold values from 1 to 2048
Outputs:
- attended: bfloat16 [32, 8192], P(('parts', 'seq')), parts along dimension 0
There are 2 independent parts, one for each index of `parts`. A program takes and returns all parts, laid end to end along the dimension named above; each array names one. Nothing has to cross between parts.
Inputs may be any that keep to these rules, and one draw needn't show every extreme that they name: Row r's list (rows 2r and 2r+1 of keep_lists) names 64 different blocks of 0 to 127.
All inputs are finite; a program needn't handle non-finite values.
Results may differ from a plain program's by a relative error of at most 0.007.
Values may be sent and summed in bfloat16 or wider, within the bound.
No kernel may reach another device: no remote copies, remote signals or barrier semaphores. Data moves between devices by JAX's collectives and lax.ppermute only.
A program may use at most 128 MiB of HBM per device.

v0:
```python
import jax
import jax.numpy as jnp
from jax import lax
from jax.sharding import PartitionSpec as P

HEADS = 64
KVH = 8
HD = 128
BLOCK = 128
NEG_BIG = -1e30


def merge_terms(first, second):
    ceiling = jnp.maximum(first[0], second[0])
    left_scale = jnp.exp(first[0] - ceiling)
    right_scale = jnp.exp(second[0] - ceiling)
    return (
        ceiling,
        left_scale * first[1] + right_scale * second[1],
        left_scale[..., None] * first[2] + right_scale[..., None] * second[2],
    )


def block_terms(scores, live_keys, value_rows, form):
    masked = jnp.where(live_keys, scores, NEG_BIG)
    block_max = jnp.max(masked, axis=-1)
    weights = jnp.where(live_keys, jnp.exp(scores - block_max[..., None]), 0.0)
    block_sum = jnp.sum(weights, axis=-1)
    block_out = jnp.einsum(
        form, weights.astype(jnp.bfloat16), value_rows, preferred_element_type=jnp.float32
    )
    global_maximum = jnp.max(block_max, axis=-1)
    factor = jnp.exp(block_max - global_maximum[..., None])
    return (
        global_maximum,
        jnp.sum(factor * block_sum, axis=-1),
        jnp.sum(factor[..., None] * block_out, axis=-2),
    )


def per_device(
    queries,
    new_keys,
    new_values,
    doc_keys,
    doc_values,
    suffix_keys,
    suffix_values,
    keep_lists,
    suffix_lengths,
):
    groups = HEADS // KVH
    factor_scale = HD ** (-0.5)
    devices = lax.axis_size("seq")
    my_index = lax.axis_index("seq")
    row_id = my_index // 2
    parity = my_index % 2
    blocks_here = doc_keys.shape[0] // BLOCK
    gathered = lax.all_gather(queries, "seq", axis=0, tiled=True)
    every_list = lax.all_gather(keep_lists, "seq", axis=0, tiled=True)
    local_ids = every_list.reshape(devices // 2, -1) - my_index * blocks_here
    block_range = jnp.arange(blocks_here, dtype=jnp.int32)
    row_hits = jnp.any(local_ids[:, :, None] == block_range[None, None, :], axis=1)
    token_mask = jnp.repeat(row_hits, 2, axis=0)
    q_heads = gathered.reshape(devices, KVH, groups, HD).transpose(1, 0, 2, 3)
    key_heads = doc_keys.reshape(blocks_here, BLOCK, KVH, HD).transpose(2, 0, 1, 3)
    value_heads = doc_values.reshape(blocks_here, BLOCK, KVH, HD).transpose(2, 0, 1, 3)

    def doc_head(head_item):
        q_part, key_part, value_part = head_item
        scores = (
            jnp.einsum("tgd,bjd->tgbj", q_part, key_part, preferred_element_type=jnp.float32)
            * factor_scale
        )
        return block_terms(scores, token_mask[:, None, :, None], value_part, "tgbj,bjd->tgbd")

    doc_max, doc_sum, doc_out = lax.map(doc_head, (q_heads, key_heads, value_heads))
    doc_partial = (
        doc_max.transpose(1, 0, 2).reshape(devices, HEADS),
        doc_sum.transpose(1, 0, 2).reshape(devices, HEADS),
        doc_out.transpose(1, 0, 2, 3).reshape(devices, HEADS, HD),
    )
    q_rows = lax.dynamic_slice_in_dim(gathered, 2 * row_id, 2, 0).reshape(2, KVH, groups, HD)
    suffix_here = suffix_keys.shape[0]
    suffix_blocks = suffix_here // BLOCK
    keys_suf = suffix_keys.reshape(suffix_blocks, BLOCK, KVH, HD)
    values_suf = suffix_values.reshape(suffix_blocks, BLOCK, KVH, HD)
    scores = (
        jnp.einsum("tkgd,bjkd->tkgbj", q_rows, keys_suf, preferred_element_type=jnp.float32)
        * factor_scale
    )
    position = parity * suffix_here + jnp.arange(suffix_here, dtype=jnp.int32).reshape(
        suffix_blocks, BLOCK
    )
    live_keys = position < suffix_lengths[row_id]
    row_partial = block_terms(scores, live_keys, values_suf, "tkgbj,bjkd->tkgbd")
    own_scores = (
        jnp.einsum(
            "tkgd,kd->tkg", q_rows, new_keys.reshape(KVH, HD), preferred_element_type=jnp.float32
        )
        * factor_scale
    )
    visible = jnp.broadcast_to(
        (jnp.arange(2, dtype=jnp.int32) >= parity)[:, None, None], own_scores.shape
    )
    own_values = jnp.broadcast_to(
        new_values.reshape(KVH, HD).astype(jnp.float32)[None, :, None, :], (2, KVH, groups, HD)
    )
    own_partial = (
        jnp.where(visible, own_scores, NEG_BIG),
        visible.astype(jnp.float32),
        jnp.where(visible[..., None], own_values, 0.0),
    )
    row_partial = merge_terms(row_partial, own_partial)
    placed = (
        lax.dynamic_update_slice(
            jnp.full((devices, HEADS), NEG_BIG, jnp.float32),
            row_partial[0].reshape(2, HEADS),
            (2 * row_id, 0),
        ),
        lax.dynamic_update_slice(
            jnp.zeros((devices, HEADS), jnp.float32),
            row_partial[1].reshape(2, HEADS),
            (2 * row_id, 0),
        ),
        lax.dynamic_update_slice(
            jnp.zeros((devices, HEADS, HD), jnp.float32),
            row_partial[2].reshape(2, HEADS, HD),
            (2 * row_id, 0, 0),
        ),
    )
    span_max, span_sum, span_out = merge_terms(doc_partial, placed)
    units = (span_out / jnp.maximum(span_sum, 1.0)[..., None]).astype(jnp.bfloat16)
    parts_max, parts_sum = (
        lax.all_to_all(span_max[:, None, :], "seq", split_axis=0, concat_axis=1, tiled=True),
        lax.all_to_all(span_sum[:, None, :], "seq", split_axis=0, concat_axis=1, tiled=True),
    )
    parts_unit = lax.all_to_all(
        units.reshape(devices, 1, HEADS * HD), "seq", split_axis=0, concat_axis=1, tiled=True
    )
    ceiling = jnp.max(parts_max, axis=1)
    weight = jnp.exp(parts_max - ceiling[:, None, :]) * parts_sum
    total_sum = jnp.sum(weight, axis=1)
    total_out = jnp.sum(
        weight[..., None] * parts_unit.reshape(1, devices, HEADS, HD).astype(jnp.float32), axis=1
    )
    return (total_out / total_sum[..., None]).reshape(1, HEADS * HD).astype(jnp.bfloat16)


def solution(mesh):
    in_specs = (
        P(("parts", "seq"), None),
        P(("parts", "seq"), None),
        P(("parts", "seq"), None),
        P(("parts", "seq"), None),
        P(("parts", "seq"), None),
        P(("parts", "seq"), None),
        P(("parts", "seq"), None),
        P(("parts", "seq"), None),
        P("parts"),
    )
    out_specs = P(("parts", "seq"), None)
    return jax.shard_map(
        per_device, mesh=mesh, in_specs=in_specs, out_specs=out_specs, check_vma=False
    )
```

profile of v0, /device:TPU:0, one launch (start us, length us, event | category | flops | bytes accessed | tf_op | source)
XLA Modules:
  0.0 115.1 jit_solution(774386942064762164)
XLA Ops:
  0.0 24.8 %all-gather.1 = bf16[16,1,8192]{2,1,0:T(2,128)(2,1)S(1)} all-gather(bf16[1,1,8192]{2,1,0:T(2,128)(2,1)} %bitcast.210), channel_id=1, replica_groups=mesh['parts'=2,'seq'=16] {'seq'}, dimensions={0}, use_global_device_ids=true | all-gather | bytes 278528 | tf_op jit(solution)/shard_map/all_gather | solution.py:59
  24.8 2.2 %copy.160 = bf16[128,8,8,128]{3,2,1,0:T(8,128)(2,1)S(1)} copy(bf16[128,8,8,128]{3,1,2,0:T(8,128)(2,1)} %bitcast.191) | data formatting | bytes 4194304
  27.2 0.2 dynamic-slice_reduce_fusion
  27.4 0.3 copy-done.11
  27.7 0.7 dynamic_slice.17
  28.4 0.7 add_compare_fusion
  29.1 0.2 fusion.47
  29.3 0.8 select_reduce_fusion.2
  30.1 0.9 fusion.38
  31.1 0.7 fusion.54
  32.1 17.4 %all-gather = s32[16,1,32]{2,1,0:T(1,128)S(1)} all-gather(s32[1,1,32]{2,1,0:T(1,128)S(1)} %bitcast.212), channel_id=1, replica_groups=mesh['parts'=2,'seq'=16] {'seq'}, dimensions={0}, use_global_device_ids=true | all-gather | bytes 2176 | tf_op jit(solution)/shard_map/all_gather | solution.py:60
  49.6 0.2 fusion.45
  49.8 1.6 %reduce.8 = bf16[16,8192]{1,0:T(8,128)(2,1)S(1)} reduce(bf16[16,1,8192]{2,1,0:T(2,128)(2,1)S(1)} %all-gather.1, bf16[]{:T(256)} %constant.83), dimensions={1}, to_apply=%all-gather.1.reduce_sub_computation | reduce | bytes 524290 | tf_op jit(solution)/shard_map/all_gather | solution.py:59
  51.5 0.6 copy.157
  52.3 0.5 copy.115
  52.8 1.1 copy-done.2
  53.9 0.6 copy.158
  54.7 1.9 %copy.116 = bf16[8,8,128,128]{3,2,1,0:T(8,128)(2,1)} copy(bf16[8,8,128,128]{3,0,2,1:T(8,128)(2,1)S(1)} %bitcast_bitcast_fusion.2) | data formatting | bytes 4194304
  56.6 20.4 %while.15 = (s32[]{:T(128)}, f32[8,16,8]{1,2,0:T(8,128)S(1)}, f32[8,16,8]{1,2,0:T(8,128)S(1)}, f32[8,16,8,128]{3,2,0,1:T(8,128)S(1)}, bf16[8,16,8,128]{3,2,0,1:T...) while((s32[]{:T(128)}, f32[8,16,8]{1,2,0:T(8,128)S(1)}, ...), condition=%wide.region_7.8_spmd.clone, body=%wide.region_1.7_spmd.clone.sunk | while | flops 68535040 | bytes 2387621 | solution.py:77
  56.6 0.4 select_reduce_fusion.5
  57.0 0.5 fusion.66
  57.7 1.3 %fusion.67 = f32[16,8,128]{2,0,1:T(8,128)S(1)} fusion(bf16[16,8,8,128]{3,1,2,0:T(8,128)(2,1)S(1)} %get-tuple-element.219, bf16[8,8,128,128]{3,2,1,0:T(8,128)(2,1)} %get-tuple-element.245, s32[]{:T(128)} %get-tuple-element.230, f32[16,8,8]{0,1,2:T(8,128)S(1)} %copy.220), kind=kOutput, calls=%fused_computation.4.clone.1 | convolution fusion | flops 33800192 | bytes 594432 | tf_op jit(solution)/shard_map/while/body/eval_jaxpr/tgbj,bjd->tgbd/dot_general | solution.py:29
  59.1 0.4 select_reduce_fusion.5
  59.5 0.5 fusion.66
  60.2 1.3 %fusion.67 = f32[16,8,128]{2,0,1:T(8,128)S(1)} fusion(bf16[16,8,8,128]{3,1,2,0:T(8,128)(2,1)S(1)} %get-tuple-element.219, bf16[8,8,128,128]{3,2,1,0:T(8,128)(2,1)} %get-tuple-element.245, s32[]{:T(128)} %get-tuple-element.230, f32[16,8,8]{0,1,2:T(8,128)S(1)} %copy.220), kind=kOutput, calls=%fused_computation.4.clone.1 | convolution fusion | flops 33800192 | bytes 594432 | tf_op jit(solution)/shard_map/while/body/eval_jaxpr/tgbj,bjd->tgbd/dot_general | solution.py:29
  61.7 0.4 select_reduce_fusion.5
  62.1 0.5 fusion.66
  62.8 1.3 %fusion.67 = f32[16,8,128]{2,0,1:T(8,128)S(1)} fusion(bf16[16,8,8,128]{3,1,2,0:T(8,128)(2,1)S(1)} %get-tuple-element.219, bf16[8,8,128,128]{3,2,1,0:T(8,128)(2,1)} %get-tuple-element.245, s32[]{:T(128)} %get-tuple-element.230, f32[16,8,8]{0,1,2:T(8,128)S(1)} %copy.220), kind=kOutput, calls=%fused_computation.4.clone.1 | convolution fusion | flops 33800192 | bytes 594432 | tf_op jit(solution)/shard_map/while/body/eval_jaxpr/tgbj,bjd->tgbd/dot_general | solution.py:29
  64.2 0.4 select_reduce_fusion.5
  64.6 0.5 fusion.66
  65.3 1.3 %fusion.67 = f32[16,8,128]{2,0,1:T(8,128)S(1)} fusion(bf16[16,8,8,128]{3,1,2,0:T(8,128)(2,1)S(1)} %get-tuple-element.219, bf16[8,8,128,128]{3,2,1,0:T(8,128)(2,1)} %get-tuple-element.245, s32[]{:T(128)} %get-tuple-element.230, f32[16,8,8]{0,1,2:T(8,128)S(1)} %copy.220), kind=kOutput, calls=%fused_computation.4.clone.1 | convolution fusion | flops 33800192 | bytes 594432 | tf_op jit(solution)/shard_map/while/body/eval_jaxpr/tgbj,bjd->tgbd/dot_general | solution.py:29
  66.8 0.4 select_reduce_fusion.5
  67.2 0.5 fusion.66
  67.8 1.3 %fusion.67 = f32[16,8,128]{2,0,1:T(8,128)S(1)} fusion(bf16[16,8,8,128]{3,1,2,0:T(8,128)(2,1)S(1)} %get-tuple-element.219, bf16[8,8,128,128]{3,2,1,0:T(8,128)(2,1)} %get-tuple-element.245, s32[]{:T(128)} %get-tuple-element.230, f32[16,8,8]{0,1,2:T(8,128)S(1)} %copy.220), kind=kOutput, calls=%fused_computation.4.clone.1 | convolution fusion | flops 33800192 | bytes 594432 | tf_op jit(solution)/shard_map/while/body/eval_jaxpr/tgbj,bjd->tgbd/dot_general | solution.py:29
  69.3 0.4 select_reduce_fusion.5
  69.7 0.5 fusion.66
  70.4 1.3 %fusion.67 = f32[16,8,128]{2,0,1:T(8,128)S(1)} fusion(bf16[16,8,8,128]{3,1,2,0:T(8,128)(2,1)S(1)} %get-tuple-element.219, bf16[8,8,128,128]{3,2,1,0:T(8,128)(2,1)} %get-tuple-element.245, s32[]{:T(128)} %get-tuple-element.230, f32[16,8,8]{0,1,2:T(8,128)S(1)} %copy.220), kind=kOutput, calls=%fused_computation.4.clone.1 | convolution fusion | flops 33800192 | bytes 594432 | tf_op jit(solution)/shard_map/while/body/eval_jaxpr/tgbj,bjd->tgbd/dot_general | solution.py:29
  71.9 0.4 select_reduce_fusion.5
  72.3 0.5 fusion.66
  72.9 1.3 %fusion.67 = f32[16,8,128]{2,0,1:T(8,128)S(1)} fusion(bf16[16,8,8,128]{3,1,2,0:T(8,128)(2,1)S(1)} %get-tuple-element.219, bf16[8,8,128,128]{3,2,1,0:T(8,128)(2,1)} %get-tuple-element.245, s32[]{:T(128)} %get-tuple-element.230, f32[16,8,8]{0,1,2:T(8,128)S(1)} %copy.220), kind=kOutput, calls=%fused_computation.4.clone.1 | convolution fusion | flops 33800192 | bytes 594432 | tf_op jit(solution)/shard_map/while/body/eval_jaxpr/tgbj,bjd->tgbd/dot_general | solution.py:29
  74.4 0.4 select_reduce_fusion.5
  74.8 0.5 fusion.66
  75.5 1.3 %fusion.67 = f32[16,8,128]{2,0,1:T(8,128)S(1)} fusion(bf16[16,8,8,128]{3,1,2,0:T(8,128)(2,1)S(1)} %get-tuple-element.219, bf16[8,8,128,128]{3,2,1,0:T(8,128)(2,1)} %get-tuple-element.245, s32[]{:T(128)} %get-tuple-element.230, f32[16,8,8]{0,1,2:T(8,128)S(1)} %copy.220), kind=kOutput, calls=%fused_computation.4.clone.1 | convolution fusion | flops 33800192 | bytes 594432 | tf_op jit(solution)/shard_map/while/body/eval_jaxpr/tgbj,bjd->tgbd/dot_general | solution.py:29
  76.9 0.3 dynamic_update_slice.20
  77.2 0.3 dynamic_update_slice.21
  77.6 0.7 copy.121
  78.2 3.4 %all-to-all-start = ((f32[16,1,64]{2,1,0:T(1,128)}), f32[16,1,64]{2,1,0:T(1,128)S(1)}, u32[]{:S(2)}, u32[]{:S(2)}) async-start(f32[16,1,64]{2,1,0:T(1,128)} %copy.121), calls=%async_computation | async-start | bytes 16384 | tf_op jit(solution)/shard_map/all_to_all | solution.py:135
  81.7 2.2 %copy.161 = bf16[128,8,8,128]{3,2,1,0:T(8,128)(2,1)S(1)} copy(bf16[128,8,8,128]{3,1,2,0:T(8,128)(2,1)} %bitcast.194) | data formatting | bytes 4194304
  84.1 0.5 copy-done.6
  84.9 0.7 fusion.31
  85.7 0.7 copy.125
  86.6 1.4 %all-to-all-done = f32[16,1,64]{2,1,0:T(1,128)S(1)} async-done(((f32[16,1,64]{2,1,0:T(1,128)}), f32[16,1,64]{2,1,0:T(1,128)S(1)}, u32[]{:S(2)}, u32[]{:S(2)}) %all-to-all-start) | async-done | bytes 4128 | tf_op jit(solution)/shard_map/all_to_all | solution.py:135
  88.0 4.6 %all-to-all-start.1 = ((f32[16,1,64]{2,1,0:T(1,128)}), f32[16,1,64]{2,1,0:T(1,128)S(1)}, u32[]{:S(2)}, u32[]{:S(2)}) async-start(f32[16,1,64]{2,1,0:T(1,128)} %copy.125), calls=%async_computation.1 | async-start | bytes 16384 | tf_op jit(solution)/shard_map/all_to_all | solution.py:136
  92.6 0.5 fusion.36
  93.2 0.6 broadcast.113
  93.8 2.3 %reduce.15 = bf16[16,8192]{1,0:T(8,128)(2,1)S(1)} reduce(bf16[16,1,8192]{2,1,0:T(2,128)(2,1)S(1)} %reshape.281, bf16[]{:T(256)} %broadcast.113), dimensions={1}, to_apply=%reshape.281.reduce_sub_computation | reduce | bytes 524290 | tf_op jit(solution)/shard_map/reshape | solution.py:139
  96.1 0.9 reshape.294
  97.0 2.0 %all-to-all-done.1 = f32[16,1,64]{2,1,0:T(1,128)S(1)} async-done(((f32[16,1,64]{2,1,0:T(1,128)}), f32[16,1,64]{2,1,0:T(1,128)S(1)}, u32[]{:S(2)}, u32[]{:S(2)}) %all-to-all-start.1) | async-done | bytes 4128 | tf_op jit(solution)/shard_map/all_to_all | solution.py:136
  99.0 4.1 %all-to-all-start.2 = ((bf16[16,2,4096]{2,1,0:T(2,128)(2,1)}), bf16[16,2,4096]{2,1,0:T(2,128)(2,1)S(1)}, u32[]{:S(2)}, u32[]{:S(2)}) async-start(bf16[16,2,4096]{2,1,0:T(2,128)(2,1)} %reshape.294), calls=%async_computation.2 | async-start | bytes 524288 | tf_op jit(solution)/shard_map/all_to_all | solution.py:138
  103.1 9.9 %all-to-all-done.2 = bf16[16,2,4096]{2,1,0:T(2,128)(2,1)S(1)} async-done(((bf16[16,2,4096]{2,1,0:T(2,128)(2,1)}), bf16[16,2,4096]{2,1,0:T(2,128)(2,1)S(1)}, u32[]{:S(2)}, u32[]{:S(2)}) %all-to-all-start.2) | async-done | bytes 262176 | tf_op jit(solution)/shard_map/all_to_all | solution.py:138
  113.0 0.3 reshape.295
  113.3 0.2 mul.151
  113.5 0.8 multiply_reduce_fusion.1
  114.4 0.7 divide_convert_fusion
  (117 shorter events, 4.5 us)
Async XLA Ops:
  0.0 29.1 %copy-start = (bf16[1,1024]{1,0:T(2,128)(2,1)S(1)}, bf16[1,1024]{1,0:T(2,128)(2,1)}, u32[]{:S(2)}) copy-start(bf16[1,1024]{1,0:T(2,128)(2,1)} %param.12) | copy-start | bytes 6148
  24.8 6.3 %copy-start.8 = (pred[2]{0:T(512)(128)(4,1)}, pred[2]{0:T(512)(128)(4,1)S(1)}, u32[]{:S(2)}) copy-start(pred[2]{0:T(512)(128)(4,1)S(1)} %get-tuple-element.152) | copy-start | bytes 10
  27.1 0.7 copy-start.11
  29.3 2.7 %copy-start.10 = (s32[1,32]{1,0:T(1,128)S(1)}, s32[1,32]{1,0:T(1,128)}, u32[]{:S(2)}) copy-start(s32[1,32]{1,0:T(1,128)} %param.18) | copy-start | bytes 388
  30.1 21.4 %copy-start.1 = (bf16[1024,1024]{1,0:T(8,128)(2,1)S(1)}, bf16[1024,1024]{1,0:T(8,128)(2,1)}, u32[]{:S(2)}) copy-start(bf16[1024,1024]{1,0:T(8,128)(2,1)} %param.14) | copy-start | bytes 6291460
  52.3 1.6 %copy-start.2 = (bf16[1024,1024]{1,0:T(8,128)(2,1)S(1)}, bf16[1024,1024]{1,0:T(8,128)(2,1)}, u32[]{:S(2)}) copy-start(bf16[1024,1024]{1,0:T(8,128)(2,1)} %param.15) | copy-start | bytes 6291460
  54.6 1.9 %copy-start.4 = (f32[8,16,8]{1,2,0:T(8,128)S(1)}, f32[8,16,8]{1,2,0:T(8,128)}, u32[]{:S(2)}) copy-start(f32[8,16,8]{1,2,0:T(8,128)} %custom-call) | copy-start | bytes 12292
  54.7 1.9 %copy-start.5 = (f32[8,16,8]{1,2,0:T(8,128)S(1)}, f32[8,16,8]{1,2,0:T(8,128)}, u32[]{:S(2)}) copy-start(f32[8,16,8]{1,2,0:T(8,128)} %custom-call.1) | copy-start | bytes 12292
  78.2 9.8 %all-to-all-start = ((f32[16,1,64]{2,1,0:T(1,128)}), f32[16,1,64]{2,1,0:T(1,128)S(1)}, u32[]{:S(2)}, u32[]{:S(2)}) async-start(f32[16,1,64]{2,1,0:T(1,128)} %copy.121), calls=%async_computation | async-start | bytes 16384 | tf_op jit(solution)/shard_map/all_to_all | solution.py:135
  83.9 0.7 copy-start.6
  83.9 0.9 copy-start.7
  83.9 1.0 copy-start.3
  84.9 0.7 copy-start.9
  88.0 10.9 %all-to-all-start.1 = ((f32[16,1,64]{2,1,0:T(1,128)}), f32[16,1,64]{2,1,0:T(1,128)S(1)}, u32[]{:S(2)}, u32[]{:S(2)}) async-start(f32[16,1,64]{2,1,0:T(1,128)} %copy.125), calls=%async_computation.1 | async-start | bytes 16384 | tf_op jit(solution)/shard_map/all_to_all | solution.py:136
  99.0 14.1 %all-to-all-start.2 = ((bf16[16,2,4096]{2,1,0:T(2,128)(2,1)}), bf16[16,2,4096]{2,1,0:T(2,128)(2,1)S(1)}, u32[]{:S(2)}, u32[]{:S(2)}) async-start(bf16[16,2,4096]{2,1,0:T(2,128)(2,1)} %reshape.294), calls=%async_computation.2 | async-start | bytes 524288 | tf_op jit(solution)/shard_map/all_to_all | solution.py:138
where the time goes:
time: 116 us; the launch traced here: 115 us
  blocking collectives  42.3 us (36%)
  local copies, waits for them, and re-layouts  18.6 us (16%)
  matrix products  15 us (13%)
  waiting for transfers between devices  13.3 us (11%)
  other arithmetic  13.2 us (11%)
  starting transfers between devices  12 us (10%)
    all_gather x1, blocking collectives, per_device(): gathered = lax.all_gather(queries, 'seq', axis=0, tiled=True)  24.8 us
    all_gather x1, blocking collectives, per_device(): every_list = lax.all_gather(keep_lists, 'seq', axis=0, tiled=True)  17.4 us
    unnamed x33, local copies, waits for them, and re-layouts  11.3 us
    dot_general x9, matrix products, block_terms(): jnp.einsum(form, weights.astype(jnp.bfloat16), value_rows, preferred_elem...  10.7 us
    all_to_all x1, waiting for transfers between devices, per_device(): lax.all_to_all(units.reshape(devices, 1, HEADS * HD), 'seq', split_axis=0...  9.94 us
    reduce_sum x9, other arithmetic, block_terms(): block_sum = jnp.sum(weights, axis=-1)  5.2 us
    all_to_all x1, starting transfers between devices, per_device(): lax.all_to_all(span_sum[:, None, :], 'seq', split_axis=0, concat_axis=1,...  4.56 us
    all_to_all x1, starting transfers between devices, per_device(): lax.all_to_all(units.reshape(devices, 1, HEADS * HD), 'seq', split_axis=0...  4.05 us
  transfers between devices with their start and end apart: 3, of which 3 were waited for; matrix products, arithmetic and copies ran while one was open for 8% of the time, Pallas kernels for 0%

commit v1 on v0

--- a/solution.py
+++ b/solution.py
@@ -56,8 +56,11 @@
     row_id = my_index // 2
     parity = my_index % 2
     blocks_here = doc_keys.shape[0] // BLOCK
-    gathered = lax.all_gather(queries, "seq", axis=0, tiled=True)
-    every_list = lax.all_gather(keep_lists, "seq", axis=0, tiled=True)
+    gathered, every_list = jnp.split(
+        lax.all_gather(jnp.concatenate([queries, keep_lists], axis=1), "seq", axis=0, tiled=True),
+        [queries.shape[1]],
+        axis=1,
+    )
     local_ids = every_list.reshape(devices // 2, -1) - my_index * blocks_here
     block_range = jnp.arange(blocks_here, dtype=jnp.int32)
     row_hits = jnp.any(local_ids[:, :, None] == block_range[None, None, :], axis=1)

time: 116 us -> 97.8 us (0.84)
  blocking collectives: 42.3 us -> 24.7 us
    all_gather x2 -> x1, blocking collectives: 42.3 us -> 24.7 us  [per_device(): lax.all_gather(jnp.concatenate([queries, keep_lists], axis=1), 'seq', axi...]
    all_gather x1 -> x0, other arithmetic: 1.62 us -> none  [per_device(): gathered = lax.all_gather(queries, 'seq', axis=0, tiled=True)]
    unnamed x33 -> x26, local copies, waits for them, and re-layouts: 11.3 us -> 11.5 us
  transfers between devices with their start and end apart: 3 -> 3, of which waited for: 3 -> 3; matrix products, arithmetic and copies ran while one was open for 8% -> 9% of each run, Pallas kernels for 0% -> 0%
where the time goes in v1:
time: 97.8 us; the launch traced here: 97.1 us
  blocking collectives  24.7 us (25%)
  local copies, waits for them, and re-layouts  18.7 us (19%)
  matrix products  14.9 us (15%)
  waiting for transfers between devices  13.4 us (14%)
  other arithmetic  12.7 us (13%)
  starting transfers between devices  12.1 us (12%)
    all_gather x1, blocking collectives, per_device(): lax.all_gather(jnp.concatenate([queries, keep_lists], axis=1), 'seq', axi...  24.7 us
    unnamed x26, local copies, waits for them, and re-layouts  11.5 us
    dot_general x9, matrix products, block_terms(): jnp.einsum(form, weights.astype(jnp.bfloat16), value_rows, preferred_elem...  10.7 us
    all_to_all x1, waiting for transfers between devices, per_device(): lax.all_to_all(units.reshape(devices, 1, HEADS * HD), 'seq', split_axis=0...  9.94 us
    reduce_sum x9, other arithmetic, block_terms(): block_sum = jnp.sum(weights, axis=-1)  5.21 us
    all_to_all x1, starting transfers between devices, per_device(): lax.all_to_all(span_sum[:, None, :], 'seq', split_axis=0, concat_axis=1,...  4.52 us
    all_to_all x1, starting transfers between devices, per_device(): lax.all_to_all(units.reshape(devices, 1, HEADS * HD), 'seq', split_axis=0...  4.05 us
    all_to_all x1, starting transfers between devices, per_device(): lax.all_to_all(span_max[:, None, :], 'seq', split_axis=0, concat_axis=1,...  3.49 us
  transfers between devices with their start and end apart: 3, of which 3 were waited for; matrix products, arithmetic and copies ran while one was open for 9% of the time, Pallas kernels for 0%

profile of v1, /device:TPU:0, one launch (start us, length us, event | category | flops | bytes accessed | tf_op | source)
XLA Modules:
  0.0 97.1 jit_solution(7833974268275504866)
XLA Ops:
  0.0 0.8 convert_element_type.58
  0.8 0.8 maximum_bitcast_fusion
  1.6 24.7 %all-gather = bf16[16,1,8224]{2,1,0:T(2,128)(2,1)S(1)} all-gather(bf16[1,1,8224]{2,1,0:T(2,128)(2,1)S(1)} %maximum_bitcast_fusion), channel_id=1, replica_groups=mesh['parts'=2,'seq'=16] {'seq'}, dimensions={0}, use_global_device_ids=true | all-gather | bytes 279616 | tf_op jit(solution)/shard_map/all_gather | solution.py:60
  26.4 0.6 copy.161
  27.1 0.1 bitcast_bitcast_fusion.1
  27.3 0.4 copy-done.6
  27.7 0.7 dynamic_slice.17
  28.4 0.7 add_compare_fusion
  29.1 0.2 fusion.46
  29.3 0.8 select_reduce_fusion.2
  30.1 1.0 fusion.38
  31.6 2.2 %copy.158 = bf16[128,8,8,128]{3,2,1,0:T(8,128)(2,1)S(1)} copy(bf16[128,8,8,128]{3,1,2,0:T(8,128)(2,1)} %bitcast.197) | data formatting | bytes 4194304
  34.0 0.5 copy.115
  34.5 1.1 %copy-done.2 = bf16[1024,1024]{1,0:T(8,128)(2,1)S(1)} copy-done((bf16[1024,1024]{1,0:T(8,128)(2,1)S(1)}, bf16[1024,1024]{1,0:T(8,128)(2,1)}, u32[]{:S(2)}) %copy-start.2) | copy-done | bytes 2097176
  35.5 0.6 copy.159
  36.3 1.9 %copy.116 = bf16[8,8,128,128]{3,2,1,0:T(8,128)(2,1)} copy(bf16[8,8,128,128]{3,0,2,1:T(8,128)(2,1)S(1)} %bitcast_bitcast_fusion.2) | data formatting | bytes 4194304
  38.2 0.3 compare_reduce_fusion
  38.5 20.4 %while.15 = (s32[]{:T(128)}, f32[8,16,8]{1,2,0:T(8,128)S(1)}, f32[8,16,8]{1,2,0:T(8,128)S(1)}, f32[8,16,8,128]{3,2,0,1:T(8,128)S(1)}, bf16[8,16,8,128]{3,2,0,1:T...) while((s32[]{:T(128)}, f32[8,16,8]{1,2,0:T(8,128)S(1)}, ...), condition=%wide.region_7.8_spmd.clone, body=%wide.region_1.7_spmd.clone.sunk | while | flops 68535040 | bytes 2387621 | solution.py:80
  38.6 0.4 select_reduce_fusion.5
  39.0 0.5 fusion.65
  39.6 1.3 %fusion.66 = f32[16,8,128]{2,0,1:T(8,128)S(1)} fusion(bf16[16,8,8,128]{3,1,2,0:T(8,128)(2,1)S(1)} %get-tuple-element.221, bf16[8,8,128,128]{3,2,1,0:T(8,128)(2,1)} %get-tuple-element.247, s32[]{:T(128)} %get-tuple-element.232, f32[16,8,8]{0,1,2:T(8,128)S(1)} %copy.223), kind=kOutput, calls=%fused_computation.4.clone.1 | convolution fusion | flops 33800192 | bytes 594432 | tf_op jit(solution)/shard_map/while/body/eval_jaxpr/tgbj,bjd->tgbd/dot_general | solution.py:29
  41.1 0.4 select_reduce_fusion.5
  41.5 0.5 fusion.65
  42.2 1.3 %fusion.66 = f32[16,8,128]{2,0,1:T(8,128)S(1)} fusion(bf16[16,8,8,128]{3,1,2,0:T(8,128)(2,1)S(1)} %get-tuple-element.221, bf16[8,8,128,128]{3,2,1,0:T(8,128)(2,1)} %get-tuple-element.247, s32[]{:T(128)} %get-tuple-element.232, f32[16,8,8]{0,1,2:T(8,128)S(1)} %copy.223), kind=kOutput, calls=%fused_computation.4.clone.1 | convolution fusion | flops 33800192 | bytes 594432 | tf_op jit(solution)/shard_map/while/body/eval_jaxpr/tgbj,bjd->tgbd/dot_general | solution.py:29
  43.6 0.4 select_reduce_fusion.5
  44.1 0.5 fusion.65
  44.7 1.3 %fusion.66 = f32[16,8,128]{2,0,1:T(8,128)S(1)} fusion(bf16[16,8,8,128]{3,1,2,0:T(8,128)(2,1)S(1)} %get-tuple-element.221, bf16[8,8,128,128]{3,2,1,0:T(8,128)(2,1)} %get-tuple-element.247, s32[]{:T(128)} %get-tuple-element.232, f32[16,8,8]{0,1,2:T(8,128)S(1)} %copy.223), kind=kOutput, calls=%fused_computation.4.clone.1 | convolution fusion | flops 33800192 | bytes 594432 | tf_op jit(solution)/shard_map/while/body/eval_jaxpr/tgbj,bjd->tgbd/dot_general | solution.py:29
  46.2 0.4 select_reduce_fusion.5
  46.6 0.5 fusion.65
  47.3 1.3 %fusion.66 = f32[16,8,128]{2,0,1:T(8,128)S(1)} fusion(bf16[16,8,8,128]{3,1,2,0:T(8,128)(2,1)S(1)} %get-tuple-element.221, bf16[8,8,128,128]{3,2,1,0:T(8,128)(2,1)} %get-tuple-element.247, s32[]{:T(128)} %get-tuple-element.232, f32[16,8,8]{0,1,2:T(8,128)S(1)} %copy.223), kind=kOutput, calls=%fused_computation.4.clone.1 | convolution fusion | flops 33800192 | bytes 594432 | tf_op jit(solution)/shard_map/while/body/eval_jaxpr/tgbj,bjd->tgbd/dot_general | solution.py:29
  48.7 0.4 select_reduce_fusion.5
  49.1 0.5 fusion.65
  49.8 1.3 %fusion.66 = f32[16,8,128]{2,0,1:T(8,128)S(1)} fusion(bf16[16,8,8,128]{3,1,2,0:T(8,128)(2,1)S(1)} %get-tuple-element.221, bf16[8,8,128,128]{3,2,1,0:T(8,128)(2,1)} %get-tuple-element.247, s32[]{:T(128)} %get-tuple-element.232, f32[16,8,8]{0,1,2:T(8,128)S(1)} %copy.223), kind=kOutput, calls=%fused_computation.4.clone.1 | convolution fusion | flops 33800192 | bytes 594432 | tf_op jit(solution)/shard_map/while/body/eval_jaxpr/tgbj,bjd->tgbd/dot_general | solution.py:29
  51.3 0.4 select_reduce_fusion.5
  51.7 0.5 fusion.65
  52.4 1.3 %fusion.66 = f32[16,8,128]{2,0,1:T(8,128)S(1)} fusion(bf16[16,8,8,128]{3,1,2,0:T(8,128)(2,1)S(1)} %get-tuple-element.221, bf16[8,8,128,128]{3,2,1,0:T(8,128)(2,1)} %get-tuple-element.247, s32[]{:T(128)} %get-tuple-element.232, f32[16,8,8]{0,1,2:T(8,128)S(1)} %copy.223), kind=kOutput, calls=%fused_computation.4.clone.1 | convolution fusion | flops 33800192 | bytes 594432 | tf_op jit(solution)/shard_map/while/body/eval_jaxpr/tgbj,bjd->tgbd/dot_general | solution.py:29
  53.8 0.4 select_reduce_fusion.5
  54.2 0.5 fusion.65
  54.9 1.3 %fusion.66 = f32[16,8,128]{2,0,1:T(8,128)S(1)} fusion(bf16[16,8,8,128]{3,1,2,0:T(8,128)(2,1)S(1)} %get-tuple-element.221, bf16[8,8,128,128]{3,2,1,0:T(8,128)(2,1)} %get-tuple-element.247, s32[]{:T(128)} %get-tuple-element.232, f32[16,8,8]{0,1,2:T(8,128)S(1)} %copy.223), kind=kOutput, calls=%fused_computation.4.clone.1 | convolution fusion | flops 33800192 | bytes 594432 | tf_op jit(solution)/shard_map/while/body/eval_jaxpr/tgbj,bjd->tgbd/dot_general | solution.py:29
  56.4 0.4 select_reduce_fusion.5
  56.8 0.5 fusion.65
  57.5 1.3 %fusion.66 = f32[16,8,128]{2,0,1:T(8,128)S(1)} fusion(bf16[16,8,8,128]{3,1,2,0:T(8,128)(2,1)S(1)} %get-tuple-element.221, bf16[8,8,128,128]{3,2,1,0:T(8,128)(2,1)} %get-tuple-element.247, s32[]{:T(128)} %get-tuple-element.232, f32[16,8,8]{0,1,2:T(8,128)S(1)} %copy.223), kind=kOutput, calls=%fused_computation.4.clone.1 | convolution fusion | flops 33800192 | bytes 594432 | tf_op jit(solution)/shard_map/while/body/eval_jaxpr/tgbj,bjd->tgbd/dot_general | solution.py:29
  58.9 0.3 dynamic_update_slice.20
  59.2 0.3 dynamic_update_slice.21
  59.5 0.7 copy.121
  60.2 3.5 %all-to-all-start = ((f32[16,1,64]{2,1,0:T(1,128)}), f32[16,1,64]{2,1,0:T(1,128)S(1)}, u32[]{:S(2)}, u32[]{:S(2)}) async-start(f32[16,1,64]{2,1,0:T(1,128)} %copy.121), calls=%async_computation | async-start | bytes 16384 | tf_op jit(solution)/shard_map/all_to_all | solution.py:138
  63.7 2.2 %copy.162 = bf16[128,8,8,128]{3,2,1,0:T(8,128)(2,1)S(1)} copy(bf16[128,8,8,128]{3,1,2,0:T(8,128)(2,1)} %bitcast.199) | data formatting | bytes 4194304
  66.3 0.4 copy-done.5
  66.7 0.3 copy-done.3
  66.9 0.7 fusion.31
  67.8 0.7 copy.125
  68.6 1.5 %all-to-all-done = f32[16,1,64]{2,1,0:T(1,128)S(1)} async-done(((f32[16,1,64]{2,1,0:T(1,128)}), f32[16,1,64]{2,1,0:T(1,128)S(1)}, u32[]{:S(2)}, u32[]{:S(2)}) %all-to-all-start) | async-done | bytes 4128 | tf_op jit(solution)/shard_map/all_to_all | solution.py:138
  70.1 4.5 %all-to-all-start.1 = ((f32[16,1,64]{2,1,0:T(1,128)}), f32[16,1,64]{2,1,0:T(1,128)S(1)}, u32[]{:S(2)}, u32[]{:S(2)}) async-start(f32[16,1,64]{2,1,0:T(1,128)} %copy.125), calls=%async_computation.1 | async-start | bytes 16384 | tf_op jit(solution)/shard_map/all_to_all | solution.py:139
  74.6 0.5 fusion.36
  75.2 0.6 broadcast.105
  75.8 2.3 %reduce.8 = bf16[16,8192]{1,0:T(8,128)(2,1)S(1)} reduce(bf16[16,1,8192]{2,1,0:T(2,128)(2,1)S(1)} %reshape.278, bf16[]{:T(256)} %broadcast.105), dimensions={1}, to_apply=%reshape.278.reduce_sub_computation | reduce | bytes 524290 | tf_op jit(solution)/shard_map/reshape | solution.py:142
  78.1 0.9 reshape.282
  79.0 2.0 %all-to-all-done.1 = f32[16,1,64]{2,1,0:T(1,128)S(1)} async-done(((f32[16,1,64]{2,1,0:T(1,128)}), f32[16,1,64]{2,1,0:T(1,128)S(1)}, u32[]{:S(2)}, u32[]{:S(2)}) %all-to-all-start.1) | async-done | bytes 4128 | tf_op jit(solution)/shard_map/all_to_all | solution.py:139
  81.0 4.1 %all-to-all-start.2 = ((bf16[16,2,4096]{2,1,0:T(2,128)(2,1)}), bf16[16,2,4096]{2,1,0:T(2,128)(2,1)S(1)}, u32[]{:S(2)}, u32[]{:S(2)}) async-start(bf16[16,2,4096]{2,1,0:T(2,128)(2,1)} %reshape.282), calls=%async_computation.2 | async-start | bytes 524288 | tf_op jit(solution)/shard_map/all_to_all | solution.py:141
  85.1 9.9 %all-to-all-done.2 = bf16[16,2,4096]{2,1,0:T(2,128)(2,1)S(1)} async-done(((bf16[16,2,4096]{2,1,0:T(2,128)(2,1)}), bf16[16,2,4096]{2,1,0:T(2,128)(2,1)S(1)}, u32[]{:S(2)}, u32[]{:S(2)}) %all-to-all-start.2) | async-done | bytes 262176 | tf_op jit(solution)/shard_map/all_to_all | solution.py:141
  95.1 0.3 reshape.283
  95.3 0.2 mul.151
  95.5 0.8 multiply_reduce_fusion.1
  96.4 0.7 divide_convert_fusion
  (110 shorter events, 4.5 us)
Async XLA Ops:
  0.0 29.1 %copy-start = (bf16[1,1024]{1,0:T(2,128)(2,1)S(1)}, bf16[1,1024]{1,0:T(2,128)(2,1)}, u32[]{:S(2)}) copy-start(bf16[1,1024]{1,0:T(2,128)(2,1)} %param.12) | copy-start | bytes 6148
  0.0 26.4 %copy-start.1 = (bf16[1024,1024]{1,0:T(8,128)(2,1)S(1)}, bf16[1024,1024]{1,0:T(8,128)(2,1)}, u32[]{:S(2)}) copy-start(bf16[1024,1024]{1,0:T(8,128)(2,1)} %param.16) | copy-start | bytes 6291460
  27.1 0.7 copy-start.6
  33.9 1.6 %copy-start.2 = (bf16[1024,1024]{1,0:T(8,128)(2,1)S(1)}, bf16[1024,1024]{1,0:T(8,128)(2,1)}, u32[]{:S(2)}) copy-start(bf16[1024,1024]{1,0:T(8,128)(2,1)} %param.15) | copy-start | bytes 6291460
  36.3 2.2 %copy-start.4 = (f32[8,16,8]{1,2,0:T(8,128)S(1)}, f32[8,16,8]{1,2,0:T(8,128)}, u32[]{:S(2)}) copy-start(f32[8,16,8]{1,2,0:T(8,128)} %custom-call) | copy-start | bytes 12292
  60.2 9.9 %all-to-all-start = ((f32[16,1,64]{2,1,0:T(1,128)}), f32[16,1,64]{2,1,0:T(1,128)S(1)}, u32[]{:S(2)}, u32[]{:S(2)}) async-start(f32[16,1,64]{2,1,0:T(1,128)} %copy.121), calls=%async_computation | async-start | bytes 16384 | tf_op jit(solution)/shard_map/all_to_all | solution.py:138
  66.0 0.7 copy-start.5
  66.0 1.0 copy-start.3
  70.1 10.9 %all-to-all-start.1 = ((f32[16,1,64]{2,1,0:T(1,128)}), f32[16,1,64]{2,1,0:T(1,128)S(1)}, u32[]{:S(2)}, u32[]{:S(2)}) async-start(f32[16,1,64]{2,1,0:T(1,128)} %copy.125), calls=%async_computation.1 | async-start | bytes 16384 | tf_op jit(solution)/shard_map/all_to_all | solution.py:139
  81.0 14.1 %all-to-all-start.2 = ((bf16[16,2,4096]{2,1,0:T(2,128)(2,1)}), bf16[16,2,4096]{2,1,0:T(2,128)(2,1)S(1)}, u32[]{:S(2)}, u32[]{:S(2)}) async-start(bf16[16,2,4096]{2,1,0:T(2,128)(2,1)} %reshape.282), calls=%async_computation.2 | async-start | bytes 524288 | tf_op jit(solution)/shard_map/all_to_all | solution.py:141
